TPU v7x, 32 devices: a whole 2x2x4 slice. The times are simulated.
32 devices in a mesh: expert: 8 (over z, core), tensor: 4 (over y, x).
Axes of the slice: x: 2, y: 2, z: 4, core: 2. Of those that a mesh axis runs over, the one named last changes fastest.
Arguments:
- residual_in: bfloat16 [1024, 3584], P('expert'), may hold values from -8 to 8
- head_outputs: bfloat16 [1024, 4096], P('expert', 'tensor'), may hold values from -6 to 6
- out_weight: bfloat16 [4096, 3584], P('tensor'), may hold values from -0.09375 to 0.09375
- gain_in: float32 [3584], replicated, may hold values from 0.25 to 1.75
- dense_gate: bfloat16 [3584, 2432], P(None, 'tensor'), may hold values from -0.09375 to 0.09375
- dense_up: bfloat16 [3584, 2432], P(None, 'tensor'), may hold values from -0.09375 to 0.09375
- dense_down: bfloat16 [2432, 3584], P('tensor'), may hold values from -0.125 to 0.125
- expert_ids: int32 [1024, 2], P('expert'), may hold values from 0 to 7, all different within a row
- route_weights: float32 [1024, 2], P('expert'), may hold values from 0.1 to 1
- gain_moe: float32 [3584], replicated, may hold values from 0.25 to 1.75
- expert_gate: bfloat16 [8, 3584, 2432], P('expert', None, 'tensor'), may hold values from -0.09375 to 0.09375
- expert_up: bfloat16 [8, 3584, 2432], P('expert', None, 'tensor'), may hold values from -0.09375 to 0.09375
- expert_down: bfloat16 [8, 2432, 3584], P('expert', 'tensor'), may hold values from -0.125 to 0.125
Outputs:
- layer_out: bfloat16 [1024, 3584], P('expert', 'tensor')
Inputs may be any that keep to these rules, and one draw needn't show every extreme that they name: `expert_ids`: each row names two different experts.
All inputs are finite; a program needn't handle non-finite values.
Results may differ from a plain program's by a relative error of at most 0.006.
Values may be sent and summed in bfloat16 or wider, within the bound.
No kernel may reach another device: no remote copies, remote signals or barrier semaphores. Data moves between devices by JAX's collectives and lax.ppermute only.
A program may use at most 64 MiB of HBM per device.

v0:
```python
import jax
import jax.numpy as jnp
from jax import lax
from jax.sharding import PartitionSpec as P

eps = 1e-05


def shards(
    residual_in,
    head_outputs,
    out_weight,
    gain_in,
    dense_gate,
    dense_up,
    dense_down,
    expert_ids,
    route_weights,
    gain_moe,
    expert_gate,
    expert_up,
    expert_down,
):
    tok_rows, model_width = residual_in.shape
    experts_count = lax.axis_size("expert")
    tensor_count = lax.axis_size("tensor")
    capacity = 2 * tok_rows // experts_count
    slot_count = experts_count * capacity
    local_cols = model_width // tensor_count
    col_start = lax.axis_index("tensor") * local_cols
    x_float = residual_in.astype(jnp.float32)
    normed = (
        x_float * lax.rsqrt(jnp.mean(x_float * x_float, axis=1, keepdims=True) + eps) * gain_in
    ).astype(jnp.bfloat16)
    dense_hidden = (
        jax.nn.silu(jnp.dot(normed, dense_gate, preferred_element_type=jnp.float32))
        * jnp.dot(normed, dense_up, preferred_element_type=jnp.float32)
    ).astype(jnp.bfloat16)
    partial_value = jnp.dot(head_outputs, out_weight, preferred_element_type=jnp.float32) + jnp.dot(
        dense_hidden, dense_down, preferred_element_type=jnp.float32
    )
    flat_ids = expert_ids.reshape(-1)
    onehot = (flat_ids[:, None] == jnp.arange(experts_count, dtype=jnp.int32)[None, :]).astype(
        jnp.int32
    )
    earlier = jnp.cumsum(onehot, axis=0) - onehot
    position = jnp.sum(earlier * onehot, axis=1)
    slot_index = jnp.where(position < capacity, flat_ids * capacity + position, -1).reshape(
        tok_rows, 2
    )
    matches = slot_index[:, :, None] == jnp.arange(slot_count, dtype=jnp.int32)[None, None, :]
    placing = jnp.sum(matches.astype(jnp.bfloat16), axis=1)
    weighing = jnp.sum(matches.astype(jnp.float32) * route_weights[:, :, None], axis=1)
    shares = lax.psum_scatter(partial_value, "tensor", scatter_dimension=1, tiled=True)
    mixed_cols = lax.dynamic_slice_in_dim(x_float, col_start, local_cols, 1) + shares
    squares = lax.psum(jnp.sum(mixed_cols * mixed_cols, axis=1), "tensor")
    gain_cols = lax.dynamic_slice_in_dim(gain_moe, col_start, local_cols, 0)
    routed_cols = (mixed_cols * lax.rsqrt(squares / model_width + eps)[:, None] * gain_cols).astype(
        jnp.bfloat16
    )
    outgoing = lax.dot_general(
        placing, routed_cols, (((0,), (0,)), ((), ())), preferred_element_type=jnp.float32
    ).astype(jnp.bfloat16)
    received = lax.all_to_all(outgoing, "expert", split_axis=0, concat_axis=0, tiled=True)
    pieces = lax.all_gather(received, "tensor", axis=1, tiled=True)
    gate_rows = expert_gate[0]
    up_rows = expert_up[0]
    gate_sum = jnp.dot(pieces, gate_rows, preferred_element_type=jnp.float32)
    up_sum = jnp.dot(pieces, up_rows, preferred_element_type=jnp.float32)
    hidden = (jax.nn.silu(gate_sum) * up_sum).astype(jnp.bfloat16)
    expert_part = jnp.dot(hidden, expert_down[0], preferred_element_type=jnp.float32)
    expert_cols = lax.psum_scatter(
        expert_part.astype(jnp.bfloat16), "tensor", scatter_dimension=1, tiled=True
    )
    returned = lax.all_to_all(expert_cols, "expert", split_axis=0, concat_axis=0, tiled=True)
    moe_out = jnp.dot(weighing, returned.astype(jnp.float32), precision=lax.Precision.HIGHEST)
    return (mixed_cols + moe_out).astype(jnp.bfloat16)


def solution(mesh):
    return jax.shard_map(
        shards,
        mesh=mesh,
        in_specs=(
            P("expert", None),
            P("expert", "tensor"),
            P("tensor", None),
            P(),
            P(None, "tensor"),
            P(None, "tensor"),
            P("tensor", None),
            P("expert", None),
            P("expert", None),
            P(),
            P("expert", None, "tensor"),
            P("expert", None, "tensor"),
            P("expert", "tensor", None),
        ),
        out_specs=P("expert", "tensor"),
        check_vma=False,
    )
```

profile of v0, /device:TPU:0, one launch (start us, length us, event | category | flops | bytes accessed | tf_op | source)
XLA Modules:
  0.0 195.3 jit_solution(13092806147728898816)
XLA Ops:
  6.5 0.0 copy-start
  6.5 0.0 reduce-scatter.5.cloned.1.call-start
  6.5 0.0 slice-start
  6.5 1.6 multiply_reduce_fusion
  8.1 0.0 copy-done
  8.2 0.0 copy-start.1
  8.2 0.0 slice-start.1
  8.2 0.0 copy-start.2
  8.2 4.3 %fusion.35 = f32[128,3584]{1,0:T(8,128)S(1)} fusion(bf16[128,1024]{1,0:T(8,128)(2,1)S(1)} %copy-done, bf16[1024,3584]{1,0:T(8,128)(2,1)} %param.15), kind=kOutput, calls=%fused_computation.49 | convolution fusion | flops 939524096 | bytes 9437184 | tf_op jit(solution)/shard_map/dot_general | solution.py:39
  12.5 0.0 slice-done
  12.5 0.0 copy-done.1
  12.5 0.0 slice-done.1
  12.5 0.0 copy-done.2
  12.5 1.4 fusion.25
  13.9 8.4 %convolution_add_fusion = f32[128,3584]{1,0:T(8,128)} fusion(f32[128,3584]{1,0:T(8,128)S(1)} %fusion.35, bf16[608,3584]{1,0:T(8,128)(2,1)} %param.19, bf16[3584,608]{0,1:T(8,128)(2,1)} %param.18, f32[128,608]{0,1:T(8,128)S(1)} %fusion.25, f32[3584]{0:T(1024)S(1)} %copy-done.2, f32[128]{0:T(128)S(1)} %add_rsqrt_fusion.1, bf16[128,3584]{1,0:T(8,128)(2,1)S(1)} %copy-done.1), kind=kOutput, calls=%fused_computation.1 | convolution fusion | flops 1118445568 | bytes 13629952 | tf_op jit(solution)/shard_map/dot_general | solution.py:39
  22.3 0.0 copy-start.3
  22.3 0.0 reduce-scatter.5.cloned.1.call-update
  22.3 0.0 all-gather.2.cloned.1.call-start
  22.4 1.4 convert_element_type.38
  23.8 0.0 copy-done.3
  23.8 0.1 copy.26
  23.9 0.1 eq.42
  24.0 0.1 eq.38
  24.2 0.6 reduce-window.6
  24.8 0.2 slice_reduce_fusion
  25.0 0.1 fusion.31
  25.1 0.1 reduce_sum.52
  25.3 0.1 copy.29
  25.4 0.1 copy.30
  25.5 0.8 dynamic_slice.7
  26.3 0.1 fusion.29
  26.4 31.8 %reduce-scatter.5.cloned.1.call-done = f32[128,896]{1,0:T(8,128)} async-done(((f32[128,3584]{1,0:T(8,128)}), f32[128,896]{1,0:T(8,128)}) %reduce-scatter.5.cloned.1.call-update) | async-done | bytes 458768 | tf_op jit(solution)/shard_map/reduce_scatter | solution.py:54
  58.2 1.3 multiply_reduce_fusion.1
  59.5 8.9 %psum.7 = f32[128]{0:T(128)S(1)} all-reduce(f32[128]{0:T(128)S(1)} %get-tuple-element.5), channel_id=1, replica_groups=mesh['expert'=8,'tensor'=4] {'tensor'}, use_global_device_ids=true, to_apply=%region_8.9 | all-reduce | flops 128 | bytes 1024 | tf_op jit(solution)/shard_map/psum | solution.py:56
  68.4 0.3 convolution_convert_fusion.1
  68.8 18.4 %all_to_all.24 = bf16[8,32,896]{2,1,0:T(8,128)(2,1)} all-to-all(bf16[8,32,896]{2,1,0:T(8,128)(2,1)S(1)} %bitcast.43), channel_id=1, replica_groups=mesh['expert'=8,'tensor'=4] {'expert'}, dimensions={0} | all-to-all | bytes 917504 | tf_op jit(solution)/shard_map/all_to_all | solution.py:64
  87.2 0.0 all-gather.2.cloned.1.call-update
  87.2 0.0 reduce-scatter.7.cloned.1.call-start
  87.3 31.1 %all-gather.2.cloned.1.call-done = bf16[256,3584]{1,0:T(8,128)(2,1)} async-done(((bf16[256,896]{1,0:T(8,128)(2,1)}), bf16[256,3584]{1,0:T(8,128)(2,1)}) %all-gather.2.cloned.1.call-update) | async-done | bytes 1835024 | tf_op jit(solution)/shard_map/all_gather | solution.py:65
  118.4 4.1 %fusion.3 = f32[256,608]{0,1:T(8,128)S(1)} fusion(bf16[256,3584]{1,0:T(8,128)(2,1)} %all-gather.2.cloned.1.call-done, bf16[1,3584,608]{1,2,0:T(8,128)(2,1)} %param.23), kind=kOutput, calls=%fused_computation.5 | convolution fusion | flops 1115684864 | bytes 6815744 | tf_op jit(solution)/shard_map/dot_general | solution.py:68
  122.5 9.2 %convolution_convert_fusion = bf16[256,3584]{1,0:T(8,128)(2,1)S(1)} fusion(bf16[1,608,3584]{2,1,0:T(8,128)(2,1)} %param.25, bf16[256,3584]{1,0:T(8,128)(2,1)} %all-gather.2.cloned.1.call-done, bf16[1,3584,608]{1,2,0:T(8,128)(2,1)} %param.24, f32[256,608]{0,1:T(8,128)S(1)} %fusion.3), kind=kOutput, calls=%fused_computation | convolution fusion | flops 2233221120 | bytes 13008896 | tf_op jit(solution)/shard_map/dot_general | solution.py:71
  131.7 0.0 copy-start.4
  131.7 2.3 %copy.31 = bf16[256,3584]{0,1:T(8,128)(2,1)} copy(bf16[256,3584]{1,0:T(8,128)(2,1)S(1)} %convolution_convert_fusion) | data formatting | bytes 3670016
  134.0 0.0 reduce-scatter.7.cloned.1.call-update
  134.0 33.2 %reduce-scatter.7.cloned.1.call-done = bf16[896,256]{1,0:T(8,128)(2,1)} async-done(((bf16[3584,256]{1,0:T(8,128)(2,1)}), bf16[896,256]{1,0:T(8,128)(2,1)}) %reduce-scatter.7.cloned.1.call-update) | async-done | bytes 458768
  167.2 2.0 %copy.32 = bf16[256,896]{1,0:T(8,128)(2,1)} copy(bf16[256,896]{0,1:T(8,128)(2,1)} %bitcast.45) | data formatting | bytes 917504
  169.2 4.6 %all-to-all-start.1 = ((bf16[8,32,896]{2,1,0:T(8,128)(2,1)}), bf16[8,32,896]{2,1,0:T(8,128)(2,1)S(1)}, u32[]{:S(2)}, u32[]{:S(2)}) async-start(bf16[8,32,896]{2,1,0:T(8,128)(2,1)} %bitcast.7), calls=%async_computation.2 | async-start | bytes 917504 | tf_op jit(solution)/shard_map/all_to_all | solution.py:75
  173.8 0.0 copy-done.4
  173.8 0.1 select_reduce_fusion
  173.9 13.8 %all-to-all-done.1 = bf16[8,32,896]{2,1,0:T(8,128)(2,1)S(1)} async-done(((bf16[8,32,896]{2,1,0:T(8,128)(2,1)}), bf16[8,32,896]{2,1,0:T(8,128)(2,1)S(1)}, u32[]{:S(2)}, u32[]{:S(2)}) %all-to-all-start.1) | async-done | bytes 458784 | tf_op jit(solution)/shard_map/all_to_all | solution.py:75
  187.7 1.1 fusion.11
  (8 shorter events, 0.1 us)
Async XLA Ops:
  6.5 1.6 copy-start
  6.5 51.6 %reduce-scatter.5.cloned.1.call-start = ((), (), s32[]{:S(2)}) async-start(), calls=%async_computation.4 | async-start | bytes 2293760 | tf_op jit(solution)/shard_map/reduce_scatter | solution.py:54
  6.5 6.0 %slice-start = ((s8[4358144]{0:T(1024)(128)(4,1)}), s8[4194304]{0:T(1024)(128)(4,1)S(1)}, s32[]{:S(2)}) async-start(s8[4358144]{0:T(1024)(128)(4,1)} %bitcast.40), calls=%async_computation.7 | async-start | bytes 8388608
  8.2 4.4 %copy-start.1 = (bf16[128,3584]{1,0:T(8,128)(2,1)S(1)}, bf16[128,3584]{1,0:T(8,128)(2,1)}, u32[]{:S(2)}) copy-start(bf16[128,3584]{1,0:T(8,128)(2,1)} %param.13) | copy-start | bytes 2752516
  8.2 4.4 %slice-start.1 = ((s8[4358144]{0:T(1024)(128)(4,1)}), s8[163840]{0:T(1024)(128)(4,1)S(1)}, s32[]{:S(2)}) async-start(s8[4358144]{0:T(1024)(128)(4,1)} %bitcast.40), calls=%async_computation.8 | async-start | bytes 327680
  8.2 4.4 %copy-start.2 = (f32[3584]{0:T(1024)S(1)}, f32[3584]{0:T(1024)}, u32[]{:S(2)}) copy-start(f32[3584]{0:T(1024)} %param.16) | copy-start | bytes 43012
  22.3 1.5 copy-start.3
  22.3 96.1 %all-gather.2.cloned.1.call-start = ((), (), s32[]{:S(2)}) async-start(), calls=%async_computation.5 | async-start | bytes 2293760 | tf_op jit(solution)/shard_map/all_gather | solution.py:65
  87.2 79.9 %reduce-scatter.7.cloned.1.call-start = ((), (), s32[]{:S(2)}) async-start(), calls=%async_computation.6 | async-start | bytes 2293760
  131.7 42.1 %copy-start.4 = (f32[128,2]{0,1:T(2,128)S(1)}, f32[128,2]{0,1:T(2,128)}, u32[]{:S(2)}) copy-start(f32[128,2]{0,1:T(2,128)} %param.21) | copy-start | bytes 3076
  169.2 18.5 %all-to-all-start.1 = ((bf16[8,32,896]{2,1,0:T(8,128)(2,1)}), bf16[8,32,896]{2,1,0:T(8,128)(2,1)S(1)}, u32[]{:S(2)}, u32[]{:S(2)}) async-start(bf16[8,32,896]{2,1,0:T(8,128)(2,1)} %bitcast.7), calls=%async_computation.2 | async-start | bytes 917504 | tf_op jit(solution)/shard_map/all_to_all | solution.py:75
Sparse Core Ops, SparseCore 0:
  22.4 35.7 reduce-scatter.4
  87.4 30.9 all-gather.1
  134.1 33.0 reduce-scatter.6
where the time goes:
time: 196 us; the launch traced here: 195 us
  waiting for transfers between devices  110 us (56%)
  matrix products  28.8 us (15%)
  blocking collectives  27.4 us (14%)
  between operations  13.3 us (7%)
  local copies, waits for them, and re-layouts  6.05 us (3%)
  other arithmetic  5.28 us (3%)
  starting transfers between devices  4.68 us (2%)
    unnamed x4, waiting for transfers between devices  33.2 us
    reduce_scatter x1, waiting for transfers between devices, shards(): lax.psum_scatter(partial_value, 'tensor', scatter_dimension=1, tiled=True)  31.8 us
    all_gather x1, waiting for transfers between devices, shards(): pieces = lax.all_gather(received, 'tensor', axis=1, tiled=True)  31.1 us
    all_to_all x1, blocking collectives, shards(): lax.all_to_all(outgoing, 'expert', split_axis=0, concat_axis=0, tiled=True)  18.4 us
    all_to_all x1, waiting for transfers between devices, shards(): lax.all_to_all(expert_cols, 'expert', split_axis=0, concat_axis=0, tiled=...  13.8 us
    dot_general x1, matrix products, shards(): jnp.dot(hidden, expert_down[0], preferred_element_type=jnp.float32)  9.19 us
    psum x1, blocking collectives, shards(): squares = lax.psum(jnp.sum(mixed_cols * mixed_cols, axis=1), 'tensor')  8.92 us
    dot_general x1, matrix products, shards(): jnp.dot(dense_hidden, dense_down, preferred_element_type=jnp.float32)  8.37 us
  transfers between devices with their start and end apart: 4, of which 4 were waited for; matrix products, arithmetic and copies ran while one was open for 2% of the time, Pallas kernels for 0%

commit v1 on v0

--- a/solution.py
+++ b/solution.py
@@ -4,6 +4,27 @@
 from jax.sharding import PartitionSpec as P
 
 eps = 1e-05
+
+
+def collect(x, axis, dim):
+    peers, index, span = (lax.axis_size(axis), lax.axis_index(axis), x.shape[dim])
+    upward = [(i, (i + 1) % peers) for i in range(peers)]
+    behind = [(i, (i - 1) % peers) for i in range(peers)]
+    filled = jnp.zeros((*x.shape[:dim], peers * span, *x.shape[dim + 1 :]), x.dtype)
+    filled = lax.dynamic_update_slice_in_dim(filled, x, index * span, axis=dim)
+    from_left = from_right = x
+    halfway = peers // 2
+    for lap in range(1, halfway + 1):
+        from_left = lax.ppermute(from_left, axis, upward)
+        filled = lax.dynamic_update_slice_in_dim(
+            filled, from_left, (index - lap) % peers * span, axis=dim
+        )
+        if lap < peers - halfway:
+            from_right = lax.ppermute(from_right, axis, behind)
+            filled = lax.dynamic_update_slice_in_dim(
+                filled, from_right, (index + lap) % peers * span, axis=dim
+            )
+    return filled
 
 
 def shards(
@@ -62,7 +83,7 @@
         placing, routed_cols, (((0,), (0,)), ((), ())), preferred_element_type=jnp.float32
     ).astype(jnp.bfloat16)
     received = lax.all_to_all(outgoing, "expert", split_axis=0, concat_axis=0, tiled=True)
-    pieces = lax.all_gather(received, "tensor", axis=1, tiled=True)
+    pieces = collect(received, "tensor", 1)
     gate_rows = expert_gate[0]
     up_rows = expert_up[0]
     gate_sum = jnp.dot(pieces, gate_rows, preferred_element_type=jnp.float32)

time: 196 us -> 196 us (level)
  waiting for transfers between devices: 110 us -> 107 us
  starting transfers between devices: 4.68 us -> 7.58 us
  local copies, waits for them, and re-layouts: 6.05 us -> 8.05 us
    all_gather x1 -> x0, waiting for transfers between devices: 31.1 us -> none  [shards(): pieces = lax.all_gather(received, 'tensor', axis=1, tiled=True)]
    ppermute x0 -> x3, waiting for transfers between devices: none -> 29.3 us  [the longest x2 19.7 us: collect(): from_left = lax.ppermute(from_left, axis, upward)]
    ppermute x0 -> x3, starting transfers between devices: none -> 2.93 us  [the longest x1 2.35 us: collect(): from_right = lax.ppermute(from_right, axis, behind)]
    unnamed x17 -> x19, local copies, waits for them, and re-layouts: 4.45 us -> 6.13 us
    unnamed x4 -> x3, waiting for transfers between devices: 33.2 us -> 31.7 us
  transfers between devices with their start and end apart: 4 -> 6, of which waited for: 4 -> 6; matrix products, arithmetic and copies ran while one was open for 2% -> 2% of each run, Pallas kernels for 0% -> 0%
where the time goes in v1:
time: 196 us
  waiting for transfers between devices  107 us (55%)
  matrix products  28.2 us (14%)
  blocking collectives  27.3 us (14%)
  between operations  13.6 us (7%)
  local copies, waits for them, and re-layouts  8.05 us (4%)
  starting transfers between devices  7.58 us (4%)
  other arithmetic  3.91 us (2%)
    reduce_scatter x1, waiting for transfers between devices, shards(): lax.psum_scatter(partial_value, 'tensor', scatter_dimension=1, tiled=True)  32.7 us
    unnamed x3, waiting for transfers between devices  31.7 us
    ppermute x2, waiting for transfers between devices, collect(): from_left = lax.ppermute(from_left, axis, upward)  19.7 us
    all_to_all x1, blocking collectives, shards(): lax.all_to_all(outgoing, 'expert', split_axis=0, concat_axis=0, tiled=True)  18.3 us
    all_to_all x1, waiting for transfers between devices, shards(): lax.all_to_all(expert_cols, 'expert', split_axis=0, concat_axis=0, tiled=...  13.8 us
    ppermute x1, waiting for transfers between devices, collect(): from_right = lax.ppermute(from_right, axis, behind)  9.57 us
    dot_general x1, matrix products, shards(): jnp.dot(hidden, expert_down[0], preferred_element_type=jnp.float32)  9.2 us
    psum x1, blocking collectives, shards(): squares = lax.psum(jnp.sum(mixed_cols * mixed_cols, axis=1), 'tensor')  8.94 us
  transfers between devices with their start and end apart: 6, of which 6 were waited for; matrix products, arithmetic and copies ran while one was open for 2% of the time, Pallas kernels for 0%

profile of v1, /device:TPU:0, one launch (start us, length us, event | category | flops | bytes accessed | tf_op | source)
XLA Modules:
  0.0 196.0 jit_solution(208001470419990178)
XLA Ops:
  6.5 0.0 copy-start
  6.5 0.0 reduce-scatter.5.cloned.1.call-start
  6.5 0.0 slice-start
  6.5 1.6 multiply_reduce_fusion
  8.1 0.0 copy-done
  8.2 0.0 copy-start.1
  8.2 0.0 slice-start.1
  8.2 0.0 copy-start.3
  8.2 4.3 %fusion.28 = f32[128,3584]{1,0:T(8,128)S(1)} fusion(bf16[128,1024]{1,0:T(8,128)(2,1)S(1)} %copy-done, bf16[1024,3584]{1,0:T(8,128)(2,1)} %param.15), kind=kOutput, calls=%fused_computation.49 | convolution fusion | flops 939524096 | bytes 9437184 | tf_op jit(solution)/shard_map/dot_general | solution.py:60
  12.5 0.0 slice-done
  12.5 0.0 copy-done.1
  12.5 0.0 slice-done.1
  12.5 0.0 copy-done.3
  12.5 1.4 fusion.18
  13.9 8.4 %convolution_add_fusion = f32[128,3584]{1,0:T(8,128)} fusion(f32[128,3584]{1,0:T(8,128)S(1)} %fusion.28, bf16[608,3584]{1,0:T(8,128)(2,1)} %param.19, bf16[3584,608]{0,1:T(8,128)(2,1)} %param.18, f32[128,608]{0,1:T(8,128)S(1)} %fusion.18, f32[3584]{0:T(1024)S(1)} %copy-done.3, f32[128]{0:T(128)S(1)} %add_rsqrt_fusion.1, bf16[128,3584]{1,0:T(8,128)(2,1)S(1)} %copy-done.1), kind=kOutput, calls=%fused_computation.1 | convolution fusion | flops 1118445568 | bytes 13629952 | tf_op jit(solution)/shard_map/dot_general | solution.py:60
  22.3 0.0 reduce-scatter.5.cloned.1.call-update
  22.3 0.0 copy-start.4
  22.3 0.0 reduce-scatter.7.cloned.1.call-start
  22.4 0.2 convert_element_type.38
  22.6 0.4 copy-done.4
  23.0 0.1 copy.26
  23.1 0.1 eq.46
  23.2 0.1 eq.42
  23.4 0.6 reduce-window.6
  24.0 0.2 slice_reduce_fusion
  24.2 0.1 fusion.24
  24.3 0.1 reduce_sum.52
  24.5 0.1 copy.29
  24.6 0.1 copy.30
  24.7 0.8 dynamic_slice.7
  25.5 0.1 fusion.22
  25.6 32.7 %reduce-scatter.5.cloned.1.call-done = f32[128,896]{1,0:T(8,128)} async-done(((f32[128,3584]{1,0:T(8,128)}), f32[128,896]{1,0:T(8,128)}) %reduce-scatter.5.cloned.1.call-update) | async-done | bytes 458768 | tf_op jit(solution)/shard_map/reduce_scatter | solution.py:75
  58.2 1.2 multiply_reduce_fusion.1
  59.4 8.9 %psum.7 = f32[128]{0:T(128)S(1)} all-reduce(f32[128]{0:T(128)S(1)} %get-tuple-element.5), channel_id=1, replica_groups=mesh['expert'=8,'tensor'=4] {'tensor'}, use_global_device_ids=true, to_apply=%region_8.9 | all-reduce | flops 128 | bytes 1024 | tf_op jit(solution)/shard_map/psum | solution.py:77
  68.3 0.3 convolution_convert_fusion.1
  68.7 18.3 %all_to_all.24 = bf16[8,32,896]{2,1,0:T(8,128)(2,1)S(1)} all-to-all(bf16[8,32,896]{2,1,0:T(8,128)(2,1)S(1)} %bitcast.43), channel_id=1, replica_groups=mesh['expert'=8,'tensor'=4] {'expert'}, dimensions={0} | all-to-all | bytes 917504 | tf_op jit(solution)/shard_map/all_to_all | solution.py:85
  87.0 0.6 collective-permute-start
  87.6 2.4 %collective-permute-start.1 = (bf16[256,896]{1,0:T(8,128)(2,1)S(1)}, bf16[256,896]{1,0:T(8,128)(2,1)S(1)}, u32[]{:S(2)}, u32[]{:S(2)}) collective-permute-start(bf16[256,896]{1,0:T(8,128)(2,1)S(1)} %bitcast.41), channel_id=1, source_target_pairs={{0,3},{1,0},{2,1},{3,2},{4,7},{5,4},{6,5},{7,6},{8,11},{9,8},{10,9... | collective-permute-start | bytes 1376264 | tf_op jit(solution)/shard_map/ppermute | solution.py:23
  90.0 11.4 %collective-permute-done = bf16[256,896]{1,0:T(8,128)(2,1)S(1)} collective-permute-done((bf16[256,896]{1,0:T(8,128)(2,1)S(1)}, bf16[256,896]{1,0:T(8,128)(2,1)S(1)}, u32[]{:S(2)}, u32[]{:S(2)}) %collective-permute-start) | collective-permute-done | bytes 458784 | tf_op jit(solution)/shard_map/ppermute | solution.py:18
  101.3 0.0 collective-permute-start.2
  101.3 0.1 broadcast_in_dim.7
  101.5 0.1 constant_dynamic-update-slice_fusion.3
  101.5 0.1 constant_dynamic-update-slice_fusion.2
  101.6 9.6 %collective-permute-done.1 = bf16[256,896]{1,0:T(8,128)(2,1)S(1)} collective-permute-done((bf16[256,896]{1,0:T(8,128)(2,1)S(1)}, bf16[256,896]{1,0:T(8,128)(2,1)S(1)}, u32[]{:S(2)}, u32[]{:S(2)}) %collective-permute-start.1) | collective-permute-done | bytes 458784 | tf_op jit(solution)/shard_map/ppermute | solution.py:23
  111.2 8.4 %collective-permute-done.2 = bf16[256,896]{1,0:T(8,128)(2,1)S(1)} collective-permute-done((bf16[256,896]{1,0:T(8,128)(2,1)S(1)}, bf16[256,896]{1,0:T(8,128)(2,1)S(1)}, u32[]{:S(2)}, u32[]{:S(2)}) %collective-permute-start.2) | collective-permute-done | bytes 458784 | tf_op jit(solution)/shard_map/ppermute | solution.py:18
  119.6 0.0 copy-start.2
  119.6 1.2 copy-done.2
  120.9 3.5 %fusion.1 = f32[256,608]{0,1:T(8,128)S(1)} fusion(bf16[256,3584]{1,0:T(8,128)(2,1)S(1)} %constant_dynamic-update-slice_fusion, bf16[1,3584,608]{1,2,0:T(8,128)(2,1)} %param.24), kind=kOutput, calls=%fused_computation.3 | convolution fusion | flops 1115684864 | bytes 6815744 | tf_op jit(solution)/shard_map/dot_general | solution.py:90
  124.4 9.2 %convolution_convert_fusion = bf16[256,3584]{1,0:T(8,128)(2,1)S(1)} fusion(bf16[1,608,3584]{2,1,0:T(8,128)(2,1)} %param.25, f32[256,608]{0,1:T(8,128)S(1)} %fusion.1, bf16[256,3584]{1,0:T(8,128)(2,1)} %copy-done.2, bf16[1,3584,608]{1,2,0:T(8,128)(2,1)} %param.23), kind=kOutput, calls=%fused_computation | convolution fusion | flops 2233221120 | bytes 13008896 | tf_op jit(solution)/shard_map/dot_general | solution.py:92
  133.6 2.3 %copy.31 = bf16[256,3584]{0,1:T(8,128)(2,1)} copy(bf16[256,3584]{1,0:T(8,128)(2,1)S(1)} %convolution_convert_fusion) | data formatting | bytes 3670016
  136.0 0.0 copy-start.5
  136.0 0.0 reduce-scatter.7.cloned.1.call-update
  136.0 31.6 %reduce-scatter.7.cloned.1.call-done = bf16[896,256]{1,0:T(8,128)(2,1)} async-done(((bf16[3584,256]{1,0:T(8,128)(2,1)}), bf16[896,256]{1,0:T(8,128)(2,1)}) %reduce-scatter.7.cloned.1.call-update) | async-done | bytes 458768
  167.6 2.0 %copy.32 = bf16[256,896]{1,0:T(8,128)(2,1)} copy(bf16[256,896]{0,1:T(8,128)(2,1)} %bitcast.45) | data formatting | bytes 917504
  169.6 4.6 %all-to-all-start.1 = ((bf16[8,32,896]{2,1,0:T(8,128)(2,1)}), bf16[8,32,896]{2,1,0:T(8,128)(2,1)S(1)}, u32[]{:S(2)}, u32[]{:S(2)}) async-start(bf16[8,32,896]{2,1,0:T(8,128)(2,1)} %bitcast.7), calls=%async_computation.2 | async-start | bytes 917504 | tf_op jit(solution)/shard_map/all_to_all | solution.py:96
  174.2 0.0 copy-done.5
  174.2 0.1 select_reduce_fusion
  174.4 13.8 %all-to-all-done.1 = bf16[8,32,896]{2,1,0:T(8,128)(2,1)S(1)} async-done(((bf16[8,32,896]{2,1,0:T(8,128)(2,1)}), bf16[8,32,896]{2,1,0:T(8,128)(2,1)S(1)}, u32[]{:S(2)}, u32[]{:S(2)}) %all-to-all-start.1) | async-done | bytes 458784 | tf_op jit(solution)/shard_map/all_to_all | solution.py:96
  188.1 1.1 fusion.5
  (10 shorter events, 0.2 us)
Async XLA Ops:
  6.5 1.6 copy-start
  6.5 51.7 %reduce-scatter.5.cloned.1.call-start = ((), (), s32[]{:S(2)}) async-start(), calls=%async_computation.4 | async-start | bytes 2293760 | tf_op jit(solution)/shard_map/reduce_scatter | solution.py:75
  6.5 6.0 %slice-start = ((s8[4358144]{0:T(1024)(128)(4,1)}), s8[4194304]{0:T(1024)(128)(4,1)S(1)}, s32[]{:S(2)}) async-start(s8[4358144]{0:T(1024)(128)(4,1)} %bitcast.38), calls=%async_computation.6 | async-start | bytes 8388608
  8.2 4.4 %copy-start.1 = (bf16[128,3584]{1,0:T(8,128)(2,1)S(1)}, bf16[128,3584]{1,0:T(8,128)(2,1)}, u32[]{:S(2)}) copy-start(bf16[128,3584]{1,0:T(8,128)(2,1)} %param.13) | copy-start | bytes 2752516
  8.2 4.4 %slice-start.1 = ((s8[4358144]{0:T(1024)(128)(4,1)}), s8[163840]{0:T(1024)(128)(4,1)S(1)}, s32[]{:S(2)}) async-start(s8[4358144]{0:T(1024)(128)(4,1)} %bitcast.38), calls=%async_computation.7 | async-start | bytes 327680
  8.2 4.4 %copy-start.3 = (f32[3584]{0:T(1024)S(1)}, f32[3584]{0:T(1024)}, u32[]{:S(2)}) copy-start(f32[3584]{0:T(1024)} %param.16) | copy-start | bytes 43012
  22.3 0.7 copy-start.4
  22.3 145.3 %reduce-scatter.7.cloned.1.call-start = ((), (), s32[]{:S(2)}) async-start(), calls=%async_computation.5 | async-start | bytes 2293760
  87.0 14.3 %collective-permute-start = (bf16[256,896]{1,0:T(8,128)(2,1)S(1)}, bf16[256,896]{1,0:T(8,128)(2,1)S(1)}, u32[]{:S(2)}, u32[]{:S(2)}) collective-permute-start(bf16[256,896]{1,0:T(8,128)(2,1)S(1)} %bitcast.40), channel_id=1, source_target_pairs={{0,1},{1,2},{2,3},{3,0},{4,5},{5,6},{6,7},{7,4},{8,9},{9,10},{10,1... | collective-permute-start | bytes 1376264 | tf_op jit(solution)/shard_map/ppermute | solution.py:18
  87.6 23.5 %collective-permute-start.1 = (bf16[256,896]{1,0:T(8,128)(2,1)S(1)}, bf16[256,896]{1,0:T(8,128)(2,1)S(1)}, u32[]{:S(2)}, u32[]{:S(2)}) collective-permute-start(bf16[256,896]{1,0:T(8,128)(2,1)S(1)} %bitcast.41), channel_id=1, source_target_pairs={{0,3},{1,0},{2,1},{3,2},{4,7},{5,4},{6,5},{7,6},{8,11},{9,8},{10,9... | collective-permute-start | bytes 1376264 | tf_op jit(solution)/shard_map/ppermute | solution.py:23
  101.3 18.3 %collective-permute-start.2 = (bf16[256,896]{1,0:T(8,128)(2,1)S(1)}, bf16[256,896]{1,0:T(8,128)(2,1)S(1)}, u32[]{:S(2)}, u32[]{:S(2)}) collective-permute-start(bf16[256,896]{1,0:T(8,128)(2,1)S(1)} %collective-permute-done), channel_id=1, source_target_pairs={{0,1},{1,2},{2,3},{3,0},{4,5},{5,6},{6,7},{7,4},{8,9},{9,10},{10,1... | collective-permute-start | bytes 1376264 | tf_op jit(solution)/shard_map/ppermute | solution.py:18
  119.6 1.3 copy-start.2
  136.0 38.3 %copy-start.5 = (f32[128,2]{0,1:T(2,128)S(1)}, f32[128,2]{0,1:T(2,128)}, u32[]{:S(2)}) copy-start(f32[128,2]{0,1:T(2,128)} %param.21) | copy-start | bytes 3076
  169.6 18.5 %all-to-all-start.1 = ((bf16[8,32,896]{2,1,0:T(8,128)(2,1)}), bf16[8,32,896]{2,1,0:T(8,128)(2,1)S(1)}, u32[]{:S(2)}, u32[]{:S(2)}) async-start(bf16[8,32,896]{2,1,0:T(8,128)(2,1)} %bitcast.7), calls=%async_computation.2 | async-start | bytes 917504 | tf_op jit(solution)/shard_map/all_to_all | solution.py:96
Sparse Core Ops, SparseCore 0:
  22.4 35.7 reduce-scatter.4
  136.1 31.4 reduce-scatter.6
